TPU v7x, 32 devices: a whole 2x2x4 slice. The times are simulated.
32 devices in a mesh: views: 4 (over z), bricks: 8 (over y, x, core).
Axes of the slice: x: 2, y: 2, z: 4, core: 2. Of those that a mesh axis runs over, the one named last changes fastest.
Arguments:
- tile_pixel: int32 [4, 8, 32], P('views', 'bricks'), may hold values from 0 to 15
- tile_voxel: int32 [4, 8, 32], P('views', 'bricks'), may hold values from 0 to 63
- tile_count: int32 [4, 8], P('views', 'bricks'), may hold values from 8 to 32, as said below
- features: bfloat16 [4, 8, 16, 64, 128], P('views', 'bricks'), may hold values from -6 to 6
- interp: bfloat16 [4, 8, 32, 128, 512], P('views', 'bricks'), may hold values from -0.5 to 0.5
- conv_weight: bfloat16 [3, 3, 3, 64, 64], replicated, may hold values from -0.15625 to 0.15625
- conv_bias: float32 [64], replicated, may hold values from -3 to 3
- smooth_coef: float32 [64, 128, 128], P('bricks', 'views'), may hold values from 0.04 to 0.16
Outputs:
- volume: bfloat16 [64, 64, 128, 128], P(None, 'bricks', 'views')
Inputs may be any that keep to these rules, and one draw needn't show every extreme that they name: `tile_count`: between 8 and 32 live tiles a device; counts are shared largely within a view group; some device has all 32 slots live in every draw.
All inputs are finite; a program needn't handle non-finite values.
Results may differ from a plain program's by a relative error of at most 0.0037.
Values may be sent and summed in bfloat16 or wider, within the bound.
A program may use at most 256 MiB of HBM per device.

v0:
```python
import jax
import jax.numpy as jnp
from jax import lax
from jax.sharding import PartitionSpec as P


def padded_2(array, sides, width):
    for axis, dim in sides:
        size, length = (lax.axis_size(axis), array.shape[dim])
        up = [(i, (i + 1) % size) for i in range(size - 1)]
        down = [(j, i) for i, j in up]
        last = lax.slice_in_dim(array, length - width, length, axis=dim)
        first = lax.slice_in_dim(array, 0, width, axis=dim)
        before = lax.ppermute(last, axis, up)
        after = lax.ppermute(first, axis, down)
        array = jnp.concatenate([before, array, after], axis=dim)
    return array


def convolve(padded, weights, conv_bias, width_x, width_y):
    depth = padded.shape[3]
    deep = jnp.pad(padded, ((0, 0), (0, 0), (0, 0), (1, 1)))
    stacked = jnp.concatenate(
        [deep[..., 0:depth], deep[..., 1 : depth + 1], deep[..., 2 : depth + 2]], axis=0
    )
    total = jnp.zeros((weights.shape[1], width_x, width_y, depth), jnp.float32)
    for shift_x in range(3):
        for shift_y in range(3):
            window = stacked[:, shift_x : shift_x + width_x, shift_y : shift_y + width_y, :]
            total = total + jnp.einsum(
                "oi,ixyz->oxyz",
                weights[shift_x * 3 + shift_y],
                window,
                preferred_element_type=jnp.float32,
            )
    return jax.nn.relu(total + conv_bias[:, None, None, None])


def smooth(beside_all, smooth_coef):
    padded = jnp.pad(beside_all, ((0, 0), (0, 0), (0, 0), (1, 1)))
    center = padded[:, 1:-1, 1:-1, 1:-1]
    beside = padded[:, 2:, 1:-1, 1:-1] + padded[:, :-2, 1:-1, 1:-1]
    beside = beside + padded[:, 1:-1, 2:, 1:-1] + padded[:, 1:-1, :-2, 1:-1]
    beside = beside + padded[:, 1:-1, 1:-1, 2:] + padded[:, 1:-1, 1:-1, :-2]
    return center + smooth_coef[None] * (beside - 6.0 * center)


def on_device(
    tile_pixel, tile_voxel, tile_count, features, interp, conv_weight, conv_bias, smooth_coef
):
    feats = features[0, 0]
    tiles = interp[0, 0]
    pixel_ids = tile_pixel[0, 0]
    voxel_ids = tile_voxel[0, 0]
    count = tile_count[0, 0]
    slots_total = tiles.shape[0]
    channels = feats.shape[1]
    pixels = feats.shape[2]
    size_x = smooth_coef.shape[0]
    size_y = smooth_coef.shape[1]
    depth = smooth_coef.shape[2]
    blocks = size_x * size_y // 4
    n_bricks = lax.axis_size("bricks")
    brick_index = lax.axis_index("bricks")
    view_index = lax.axis_index("views")
    sender = view_index * n_bricks + brick_index
    offset = jnp.remainder(sender * 37, slots_total)
    slot_ids = jnp.arange(slots_total, dtype=jnp.int32)
    live = jnp.remainder(slot_ids - offset, slots_total) < count
    target = (
        live[:, None] & (voxel_ids[:, None] == jnp.arange(blocks, dtype=jnp.int32)[None, :])
    ).astype(jnp.bfloat16)
    selector = (pixel_ids[:, None] == jnp.arange(feats.shape[0], dtype=jnp.int32)[None, :]).astype(
        jnp.bfloat16
    )
    chosen = jnp.einsum(
        "dk,kq->dq",
        selector,
        feats.reshape(feats.shape[0], channels * pixels),
        preferred_element_type=jnp.float32,
    )
    chosen = chosen.astype(jnp.bfloat16).reshape(slots_total, channels, pixels)
    partial_value = jnp.einsum(
        "dcp,dpv->dcv", chosen, tiles, preferred_element_type=jnp.float32
    ).astype(jnp.bfloat16)
    got_part, got_target = (
        lax.all_to_all(partial_value, ("views", "bricks"), split_axis=0, concat_axis=0, tiled=True),
        lax.all_to_all(target, ("views", "bricks"), split_axis=0, concat_axis=0, tiled=True),
    )
    lifted = jnp.einsum("sb,scv->cbv", got_target, got_part, preferred_element_type=jnp.float32)
    lifted = lifted.reshape(channels, size_x, size_y, depth)
    rectified = jax.nn.relu(lifted).astype(jnp.bfloat16)
    weights = jnp.transpose(conv_weight, (0, 1, 3, 2, 4)).reshape(9, channels, 3 * channels)
    padded = padded_2(rectified, (("views", 2), ("bricks", 1)), 1)
    gated = convolve(padded, weights, conv_bias, size_x, size_y)
    beside_all = padded_2(gated, (("views", 2), ("bricks", 1)), 1)
    return smooth(beside_all, smooth_coef).astype(jnp.bfloat16)


def solution(mesh):
    in_specs = (
        P("views", "bricks", None),
        P("views", "bricks", None),
        P("views", "bricks"),
        P("views", "bricks", None, None, None),
        P("views", "bricks", None, None, None),
        P(),
        P(),
        P("bricks", "views", None),
    )
    out_specs = P(None, "bricks", "views", None)
    return jax.shard_map(
        on_device, mesh=mesh, in_specs=in_specs, out_specs=out_specs, check_vma=False
    )
```

profile of v0, /device:TPU:1, one launch (start us, length us, event | category | flops | bytes accessed | tf_op | source)
XLA Modules:
  0.0 274.3 jit_solution(16275346424732691299)
XLA Ops:
  0.7 1.4 and_convert_fusion
  2.1 7.1 %all-to-all-start.1 = ((bf16[32,1,64]{2,1,0:T(2,128)(2,1)}), bf16[32,1,64]{2,1,0:T(2,128)(2,1)S(1)}, u32[]{:S(2)}, u32[]{:S(2)}) async-start(bf16[32,1,64]{2,1,0:T(2,128)(2,1)} %and_convert_fusion), calls=%async_computation.1 | async-start | bytes 32768 | tf_op jit(solution)/shard_map/all_to_all | solution.py:88
  9.2 1.3 fusion.34
  10.5 0.1 copy.78
  10.6 2.9 %fusion.31 = bf16[32,64,512]{2,1,0:T(8,128)(2,1)S(1)} fusion(bf16[32,64,128]{2,1,0:T(8,128)(2,1)S(1)} %bitcast.103, bf16[1,1,32,128,512]{4,3,2,1,0:T(8,128)(2,1)} %param.12), kind=kOutput, calls=%fused_computation.53 | convolution fusion | flops 269484032 | bytes 6815744 | tf_op jit(solution)/shard_map/dcp,dpv->dcv/dot_general | solution.py:83
  13.5 2.3 all-to-all-done.1
  15.9 51.0 %all_to_all.14 = bf16[32,64,512]{2,1,0:T(8,128)(2,1)S(1)} all-to-all(bf16[32,64,512]{2,1,0:T(8,128)(2,1)S(1)} %fusion.31), channel_id=1, replica_groups=mesh['views'=4,'bricks'=8] {'views','bricks'}, dimensions={0} | all-to-all | bytes 4194304 | tf_op jit(solution)/shard_map/all_to_all | solution.py:87
  66.9 4.0 %fusion.27 = bf16[64,64,512]{2,1,0:T(8,128)(2,1)} fusion(bf16[32,64,512]{2,1,0:T(8,128)(2,1)S(1)} %all_to_all.14, bf16[32,1,64]{2,1,0:T(2,128)(2,1)S(1)} %all-to-all-done.1), kind=kOutput, calls=%fused_computation.49 | convolution fusion | flops 138412032 | bytes 6295552 | tf_op jit(solution)/shard_map/sb,scv->cbv/dot_general | solution.py:90
  70.9 7.5 %convert_element_type.38 = bf16[64,8,32,128]{3,2,1,0:T(8,128)(2,1)} reshape(bf16[64,64,512]{2,1,0:T(8,128)(2,1)} %fusion.27) | data formatting | bytes 8388608 | tf_op jit(solution)/shard_map/convert_element_type | solution.py:92
  78.4 2.1 fusion.47
  80.5 0.1 copy.90
  80.6 3.4 %collective-permute-start = (bf16[64,8,1,128]{3,0,2,1:T(8,128)(2,1)S(1)}, bf16[64,8,1,128]{3,0,2,1:T(8,128)(2,1)S(1)}, u32[]{:S(2)}, u32[]{:S(2)}) collective-permute-start(bf16[64,8,1,128]{3,0,2,1:T(8,128)(2,1)S(1)} %copy.90), channel_id=1, source_target_pairs={{0,8},{8,16},{16,24},{1,9},{9,17},{17,25},{2,10},{10,18},{18,26},{... | collective-permute-start | bytes 393224 | tf_op jit(solution)/shard_map/ppermute | solution.py:14
  83.9 0.1 copy.91
  84.0 1.3 collective-permute-start.1
  85.3 1.1 collective-permute-done
  86.4 5.2 %constant_dynamic-update-slice_fusion.1 = bf16[64,8,34,128]{3,0,2,1:T(8,128)(2,1)S(1)} fusion(bf16[64,8,34,128]{3,0,2,1:T(8,128)(2,1)S(1)} %constant_dynamic-update-slice_fusion.2, bf16[64,8,32,128]{3,2,1,0:T(8,128)(2,1)} %convert_element_type.38), kind=kLoop, calls=%fused_computation.72 | loop fusion | bytes 8388608
  91.6 2.1 copy-done.1
  93.7 0.1 fusion.46
  93.8 4.2 %collective-permute-start.2 = (bf16[64,1,34,128]{3,0,2,1:T(8,128)(2,1)S(1)}, bf16[64,1,34,128]{3,0,2,1:T(8,128)(2,1)S(1)}, u32[]{:S(2)}, u32[]{:S(2)}) collective-permute-start(bf16[64,1,34,128]{3,0,2,1:T(8,128)(2,1)S(1)} %get-tuple-element.11), channel_id=1, source_target_pairs={{0,1},{1,2},{2,3},{3,4},{4,5},{5,6},{6,7},{8,9},{9,10},{10,11},{11... | collective-permute-start | bytes 1671176 | tf_op jit(solution)/shard_map/ppermute | solution.py:14
  98.0 2.1 collective-permute-start.3
  100.1 1.0 copy.47
  101.1 3.4 %collective-permute-done.2 = bf16[64,1,34,128]{3,0,2,1:T(8,128)(2,1)S(1)} collective-permute-done((bf16[64,1,34,128]{3,0,2,1:T(8,128)(2,1)S(1)}, bf16[64,1,34,128]{3,0,2,1:T(8,128)(2,1)S(1)}, u32[]{:S(2)}, u32[]{:S(2)}) %collective-permute-start.2) | collective-permute-done | bytes 557088 | tf_op jit(solution)/shard_map/ppermute | solution.py:14
  104.4 6.9 %collective-permute-done.3 = bf16[64,1,34,128]{3,0,2,1:T(8,128)(2,1)S(1)} collective-permute-done((bf16[64,1,34,128]{3,0,2,1:T(8,128)(2,1)S(1)}, bf16[64,1,34,128]{3,0,2,1:T(8,128)(2,1)S(1)}, u32[]{:S(2)}, u32[]{:S(2)}) %collective-permute-start.3) | collective-permute-done | bytes 557088 | tf_op jit(solution)/shard_map/ppermute | solution.py:15
  111.3 11.4 %select_maximum_fusion.4 = bf16[64,10,34,130]{3,0,2,1:T(8,128)(2,1)S(1)} fusion(bf16[64,1,34,128]{3,0,2,1:T(8,128)(2,1)S(1)} %collective-permute-done.3, bf16[64,8,34,128]{3,0,2,1:T(8,128)(2,1)} %copy-done.1, bf16[64,1,34,128]{3,0,2,1:T(8,128)(2,1)S(1)} %collective-permute-done.2), kind=kLoop, calls=%fused_computation.26 | loop fusion | flops 33945600 | bytes 11228160 | tf_op jit(solution)/shard_map/concatenate | solution.py:16
  122.8 6.0 %fusion.44 = (bf16[64,10,34,128]{3,0,2,1:T(8,128)(2,1)}, bf16[64,10,34,128]{3,0,2,1:T(8,128)(2,1)}) fusion(bf16[64,10,34,130]{3,0,2,1:T(8,128)(2,1)S(1)} %select_maximum_fusion.4), kind=kLoop, calls=%fused_computation.82 | loop fusion | bytes 22282240 | tf_op jit(solution)/shard_map/slice | solution.py:24
  128.7 9.4 %pad_maximum_fusion = bf16[192,10,34,128]{3,0,2,1:T(8,128)(2,1)S(1)} fusion(bf16[64,10,34,128]{3,0,2,1:T(8,128)(2,1)} %get-tuple-element.6, bf16[64,1,34,128]{3,0,2,1:T(8,128)(2,1)S(1)} %collective-permute-done.3, bf16[64,8,34,128]{3,0,2,1:T(8,128)(2,1)S(1)} %bitcast.102, bf16[64,1,34,128]{3,0,2,1:T(8,128)(2,1)S(1)} %collective-permute-done.2, ...), kind=kLoop, calls=%fused_computation.7 | loop fusion | flops 83558400 | bytes 33423360 | tf_op jit(solution)/shard_map/concatenate | solution.py:23
  138.1 0.0 copy-start.2
  138.2 6.3 %fusion.3 = f32[8,32,128,64]{2,3,1,0:T(8,128)} fusion(bf16[192,10,34,128]{3,0,2,1:T(8,128)(2,1)S(1)} %pad_maximum_fusion, bf16[9,64,192]{1,2,0:T(8,128)(2,1)} %bitcast.104), kind=kOutput, calls=%fused_computation.10 | convolution fusion | flops 805306368 | bytes 21020672 | tf_op jit(solution)/shard_map/oi,ixyz->oxyz/dot_general | solution.py:30
  144.5 4.6 %fusion.5 = f32[8,32,128,64]{2,3,1,0:T(8,128)} fusion(bf16[192,10,34,128]{3,0,2,1:T(8,128)(2,1)S(1)} %pad_maximum_fusion, bf16[9,64,192]{1,2,0:T(8,128)(2,1)S(1)} %bitcast.105), kind=kOutput, calls=%fused_computation.12 | convolution fusion | flops 805306368 | bytes 21020672 | tf_op jit(solution)/shard_map/oi,ixyz->oxyz/dot_general | solution.py:30
  149.1 4.7 %fusion.7 = f32[8,32,128,64]{2,3,1,0:T(8,128)} fusion(bf16[192,10,34,128]{3,0,2,1:T(8,128)(2,1)S(1)} %pad_maximum_fusion, bf16[9,64,192]{1,2,0:T(8,128)(2,1)S(1)} %bitcast.106), kind=kOutput, calls=%fused_computation.14 | convolution fusion | flops 805306368 | bytes 21020672 | tf_op jit(solution)/shard_map/oi,ixyz->oxyz/dot_general | solution.py:30
  153.8 4.6 %fusion.9 = f32[8,32,128,64]{2,3,1,0:T(8,128)} fusion(bf16[192,10,34,128]{3,0,2,1:T(8,128)(2,1)S(1)} %pad_maximum_fusion, bf16[9,64,192]{1,2,0:T(8,128)(2,1)S(1)} %bitcast.107), kind=kOutput, calls=%fused_computation.16 | convolution fusion | flops 805306368 | bytes 21020672 | tf_op jit(solution)/shard_map/oi,ixyz->oxyz/dot_general | solution.py:30
  158.4 4.7 %fusion.11 = f32[8,32,128,64]{2,3,1,0:T(8,128)} fusion(bf16[192,10,34,128]{3,0,2,1:T(8,128)(2,1)S(1)} %pad_maximum_fusion, bf16[9,64,192]{1,2,0:T(8,128)(2,1)S(1)} %bitcast.108), kind=kOutput, calls=%fused_computation.18 | convolution fusion | flops 805306368 | bytes 21020672 | tf_op jit(solution)/shard_map/oi,ixyz->oxyz/dot_general | solution.py:30
  163.1 4.7 %fusion.13 = f32[8,32,128,64]{2,3,1,0:T(8,128)} fusion(bf16[192,10,34,128]{3,0,2,1:T(8,128)(2,1)S(1)} %pad_maximum_fusion, bf16[9,64,192]{1,2,0:T(8,128)(2,1)S(1)} %bitcast.109), kind=kOutput, calls=%fused_computation.20 | convolution fusion | flops 805306368 | bytes 21020672 | tf_op jit(solution)/shard_map/oi,ixyz->oxyz/dot_general | solution.py:30
  167.7 4.7 %fusion.15 = f32[8,32,128,64]{2,3,1,0:T(8,128)} fusion(bf16[192,10,34,128]{3,0,2,1:T(8,128)(2,1)S(1)} %pad_maximum_fusion, bf16[9,64,192]{1,2,0:T(8,128)(2,1)S(1)} %bitcast.110), kind=kOutput, calls=%fused_computation.22 | convolution fusion | flops 805306368 | bytes 21020672 | tf_op jit(solution)/shard_map/oi,ixyz->oxyz/dot_general | solution.py:30
  172.4 4.6 %fusion.17 = f32[8,32,128,64]{2,3,1,0:T(8,128)} fusion(bf16[192,10,34,128]{3,0,2,1:T(8,128)(2,1)S(1)} %pad_maximum_fusion, bf16[9,64,192]{1,2,0:T(8,128)(2,1)S(1)} %bitcast.111), kind=kOutput, calls=%fused_computation.24 | convolution fusion | flops 805306368 | bytes 21020672 | tf_op jit(solution)/shard_map/oi,ixyz->oxyz/dot_general | solution.py:30
  177.0 25.9 %maximum_bitcast_fusion = f32[64,8,32,128]{3,0,2,1:T(8,128)S(1)} fusion(f32[8,32,128,64]{2,3,1,0:T(8,128)} %fusion.3, f32[8,32,128,64]{2,3,1,0:T(8,128)} %fusion.5, f32[8,32,128,64]{2,3,1,0:T(8,128)} %fusion.7, f32[8,32,128,64]{2,3,1,0:T(8,128)} %fusion.9, f32[8,32,128,64]{2,3,1,0:T(8,128)} %fusion.11, f32[8,32,128,64]{2,3,1,0:T(8,128)} %fusion.13, ...), kind=kOutput, calls=%fused_computation.47 | convolution fusion | flops 826277888 | bytes 88130048 | tf_op jit(solution)/shard_map/oi,ixyz->oxyz/dot_general | solution.py:30
  203.0 4.1 %collective-permute-start.4 = (f32[64,8,1,128]{3,0,2,1:T(8,128)S(1)}, f32[64,8,1,128]{3,0,2,1:T(8,128)S(1)}, u32[]{:S(2)}, u32[]{:S(2)}) collective-permute-start(f32[64,8,1,128]{3,0,2,1:T(8,128)S(1)} %get-tuple-element.9), channel_id=1, source_target_pairs={{0,8},{8,16},{16,24},{1,9},{9,17},{17,25},{2,10},{10,18},{18,26},{... | collective-permute-start | bytes 786440 | tf_op jit(solution)/shard_map/ppermute | solution.py:14
  207.1 1.3 collective-permute-start.5
  208.4 2.0 collective-permute-done.4
  210.4 3.8 %collective-permute-done.5 = f32[64,8,1,128]{3,0,2,1:T(8,128)S(1)} collective-permute-done((f32[64,8,1,128]{3,0,2,1:T(8,128)S(1)}, f32[64,8,1,128]{3,0,2,1:T(8,128)S(1)}, u32[]{:S(2)}, u32[]{:S(2)}) %collective-permute-start.5) | collective-permute-done | bytes 262176 | tf_op jit(solution)/shard_map/ppermute | solution.py:15
  214.2 0.1 pad_maximum_fusion.9
  214.4 5.6 %collective-permute-start.7 = (f32[64,1,34,128]{3,0,2,1:T(8,128)S(1)}, f32[64,1,34,128]{3,0,2,1:T(8,128)S(1)}, u32[]{:S(2)}, u32[]{:S(2)}) collective-permute-start(f32[64,1,34,128]{3,0,2,1:T(8,128)S(1)} %get-tuple-element.7), channel_id=1, source_target_pairs={{0,1},{1,2},{2,3},{3,4},{4,5},{5,6},{6,7},{8,9},{9,10},{10,11},{11... | collective-permute-start | bytes 3342344 | tf_op jit(solution)/shard_map/ppermute | solution.py:14
  220.0 2.1 collective-permute-start.6
  222.1 10.4 %collective-permute-done.7 = f32[64,1,34,128]{3,0,2,1:T(8,128)S(1)} collective-permute-done((f32[64,1,34,128]{3,0,2,1:T(8,128)S(1)}, f32[64,1,34,128]{3,0,2,1:T(8,128)S(1)}, u32[]{:S(2)}, u32[]{:S(2)}) %collective-permute-start.7) | collective-permute-done | bytes 1114144 | tf_op jit(solution)/shard_map/ppermute | solution.py:14
  232.4 11.7 %collective-permute-done.6 = f32[64,1,34,128]{3,0,2,1:T(8,128)S(1)} collective-permute-done((f32[64,1,34,128]{3,0,2,1:T(8,128)S(1)}, f32[64,1,34,128]{3,0,2,1:T(8,128)S(1)}, u32[]{:S(2)}, u32[]{:S(2)}) %collective-permute-start.6) | collective-permute-done | bytes 1114144 | tf_op jit(solution)/shard_map/ppermute | solution.py:15
  244.1 13.8 %select_maximum_fusion = f32[64,10,34,130]{3,0,2,1:T(8,128)} fusion(f32[64,1,34,128]{3,0,2,1:T(8,128)S(1)} %collective-permute-done.6, f32[64,1,34,128]{3,0,2,1:T(8,128)S(1)} %collective-permute-done.7, f32[64,8,1,128]{3,0,2,1:T(8,128)S(1)} %collective-permute-done.5, f32[64,8,32,128]{3,0,2,1:T(8,128)S(1)} %maximum_bitcast_fusion, ...), kind=kLoop, calls=%fused_computation.2 | loop fusion | flops 33945600 | bytes 22456320 | tf_op jit(solution)/shard_map/concatenate | solution.py:16
  257.9 11.6 %fusion.23 = bf16[64,8,32,128]{3,0,2,1:T(8,128)(2,1)S(1)} fusion(f32[64,8,32,128]{3,0,2,1:T(8,128)S(1)} %maximum_bitcast_fusion, f32[64,10,34,130]{3,0,2,1:T(8,128)} %select_maximum_fusion, f32[64,8,1,128]{3,0,2,1:T(8,128)S(1)} %collective-permute-done.4, f32[64,8,1,128]{3,0,2,1:T(8,128)S(1)} %collective-permute-done.5, ...), kind=kLoop, calls=%fused_computation.34 | loop fusion | flops 37748736 | bytes 32243712 | tf_op jit(solution)/shard_map/convert_element_type | solution.py:97
  269.6 4.7 %copy.57 = bf16[64,8,32,128]{3,2,1,0:T(8,128)(2,1)} copy(bf16[64,8,32,128]{3,0,2,1:T(8,128)(2,1)S(1)} %fusion.23) | data formatting | bytes 8388608 | tf_op jit(solution)/shard_map/convert_element_type | solution.py:97
  (20 shorter events, 0.1 us)
Async XLA Ops:
  2.1 13.8 %all-to-all-start.1 = ((bf16[32,1,64]{2,1,0:T(2,128)(2,1)}), bf16[32,1,64]{2,1,0:T(2,128)(2,1)S(1)}, u32[]{:S(2)}, u32[]{:S(2)}) async-start(bf16[32,1,64]{2,1,0:T(2,128)(2,1)} %and_convert_fusion), calls=%async_computation.1 | async-start | bytes 32768 | tf_op jit(solution)/shard_map/all_to_all | solution.py:88
  78.4 21.7 %copy-start.3 = (bf16[3,3,3,64,64]{4,3,2,1,0:T(8,128)(2,1)S(1)}, bf16[3,3,3,64,64]{4,3,2,1,0:T(8,128)(2,1)}, u32[]{:S(2)}) copy-start(bf16[3,3,3,64,64]{4,3,2,1,0:T(8,128)(2,1)} %param.13) | copy-start | bytes 663556
  80.6 5.8 %collective-permute-start = (bf16[64,8,1,128]{3,0,2,1:T(8,128)(2,1)S(1)}, bf16[64,8,1,128]{3,0,2,1:T(8,128)(2,1)S(1)}, u32[]{:S(2)}, u32[]{:S(2)}) collective-permute-start(bf16[64,8,1,128]{3,0,2,1:T(8,128)(2,1)S(1)} %copy.90), channel_id=1, source_target_pairs={{0,8},{8,16},{16,24},{1,9},{9,17},{17,25},{2,10},{10,18},{18,26},{... | collective-permute-start | bytes 393224 | tf_op jit(solution)/shard_map/ppermute | solution.py:14
  84.0 7.5 %collective-permute-start.1 = (bf16[64,8,1,128]{3,0,2,1:T(8,128)(2,1)S(1)}, bf16[64,8,1,128]{3,0,2,1:T(8,128)(2,1)S(1)}, u32[]{:S(2)}, u32[]{:S(2)}) collective-permute-start(bf16[64,8,1,128]{3,0,2,1:T(8,128)(2,1)S(1)} %copy.91), channel_id=1, source_target_pairs={{8,0},{16,8},{24,16},{9,1},{17,9},{25,17},{10,2},{18,10},{26,18},{... | collective-permute-start | bytes 393224 | tf_op jit(solution)/shard_map/ppermute | solution.py:15
  91.6 2.1 copy-start.1
  93.8 10.7 %collective-permute-start.2 = (bf16[64,1,34,128]{3,0,2,1:T(8,128)(2,1)S(1)}, bf16[64,1,34,128]{3,0,2,1:T(8,128)(2,1)S(1)}, u32[]{:S(2)}, u32[]{:S(2)}) collective-permute-start(bf16[64,1,34,128]{3,0,2,1:T(8,128)(2,1)S(1)} %get-tuple-element.11), channel_id=1, source_target_pairs={{0,1},{1,2},{2,3},{3,4},{4,5},{5,6},{6,7},{8,9},{9,10},{10,11},{11... | collective-permute-start | bytes 1671176 | tf_op jit(solution)/shard_map/ppermute | solution.py:14
  98.0 13.3 %collective-permute-start.3 = (bf16[64,1,34,128]{3,0,2,1:T(8,128)(2,1)S(1)}, bf16[64,1,34,128]{3,0,2,1:T(8,128)(2,1)S(1)}, u32[]{:S(2)}, u32[]{:S(2)}) collective-permute-start(bf16[64,1,34,128]{3,0,2,1:T(8,128)(2,1)S(1)} %get-tuple-element.12), channel_id=1, source_target_pairs={{1,0},{2,1},{3,2},{4,3},{5,4},{6,5},{7,6},{9,8},{10,9},{11,10},{12... | collective-permute-start | bytes 1671176 | tf_op jit(solution)/shard_map/ppermute | solution.py:15
  111.3 17.4 %slice-start = ((s8[4456448]{0:T(1024)(128)(4,1)}), s8[4194304]{0:T(1024)(128)(4,1)S(1)}, s32[]{:S(2)}) async-start(s8[4456448]{0:T(1024)(128)(4,1)} %bitcast.101), calls=%async_computation.2 | async-start | bytes 8388608
  122.8 6.0 %slice-start.1 = ((s8[4456448]{0:T(1024)(128)(4,1)}), s8[262144]{0:T(1024)(128)(4,1)S(1)}, s32[]{:S(2)}) async-start(s8[4456448]{0:T(1024)(128)(4,1)} %bitcast.101), calls=%async_computation.3 | async-start | bytes 524288
  138.1 34.2 %copy-start = (bf16[192,10,34,128]{3,0,2,1:T(8,128)(2,1)}, bf16[192,10,34,128]{3,0,2,1:T(8,128)(2,1)S(1)}, u32[]{:S(2)}) copy-start(bf16[192,10,34,128]{3,0,2,1:T(8,128)(2,1)S(1)} %pad_maximum_fusion) | copy-start | bytes 50135044
  138.1 6.4 %copy-start.2 = (bf16[3,3,64,3,64]{2,4,3,1,0:T(8,128)(2,1)S(1)}, bf16[3,3,64,3,64]{2,4,3,1,0:T(8,128)(2,1)}, u32[]{:S(2)}) copy-start(bf16[3,3,64,3,64]{2,4,3,1,0:T(8,128)(2,1)} %copy.47) | copy-start | bytes 663556
  172.4 4.7 %copy-start.5 = (f32[64]{0:T(128)S(1)}, f32[64]{0:T(128)}, u32[]{:S(2)}) copy-start(f32[64]{0:T(128)} %param.14) | copy-start | bytes 772
  203.0 7.4 %collective-permute-start.4 = (f32[64,8,1,128]{3,0,2,1:T(8,128)S(1)}, f32[64,8,1,128]{3,0,2,1:T(8,128)S(1)}, u32[]{:S(2)}, u32[]{:S(2)}) collective-permute-start(f32[64,8,1,128]{3,0,2,1:T(8,128)S(1)} %get-tuple-element.9), channel_id=1, source_target_pairs={{0,8},{8,16},{16,24},{1,9},{9,17},{17,25},{2,10},{10,18},{18,26},{... | collective-permute-start | bytes 786440 | tf_op jit(solution)/shard_map/ppermute | solution.py:14
  207.1 7.1 %collective-permute-start.5 = (f32[64,8,1,128]{3,0,2,1:T(8,128)S(1)}, f32[64,8,1,128]{3,0,2,1:T(8,128)S(1)}, u32[]{:S(2)}, u32[]{:S(2)}) collective-permute-start(f32[64,8,1,128]{3,0,2,1:T(8,128)S(1)} %get-tuple-element.10), channel_id=1, source_target_pairs={{8,0},{16,8},{24,16},{9,1},{17,9},{25,17},{10,2},{18,10},{26,18},{... | collective-permute-start | bytes 786440 | tf_op jit(solution)/shard_map/ppermute | solution.py:15
  214.4 18.0 %collective-permute-start.7 = (f32[64,1,34,128]{3,0,2,1:T(8,128)S(1)}, f32[64,1,34,128]{3,0,2,1:T(8,128)S(1)}, u32[]{:S(2)}, u32[]{:S(2)}) collective-permute-start(f32[64,1,34,128]{3,0,2,1:T(8,128)S(1)} %get-tuple-element.7), channel_id=1, source_target_pairs={{0,1},{1,2},{2,3},{3,4},{4,5},{5,6},{6,7},{8,9},{9,10},{10,11},{11... | collective-permute-start | bytes 3342344 | tf_op jit(solution)/shard_map/ppermute | solution.py:14
  220.0 38.0 %copy-start.4 = (f32[8,32,128]{2,1,0:T(8,128)S(1)}, f32[8,32,128]{2,1,0:T(8,128)}, u32[]{:S(2)}) copy-start(f32[8,32,128]{2,1,0:T(8,128)} %param.15) | copy-start | bytes 393220
  220.0 24.1 %collective-permute-start.6 = (f32[64,1,34,128]{3,0,2,1:T(8,128)S(1)}, f32[64,1,34,128]{3,0,2,1:T(8,128)S(1)}, u32[]{:S(2)}, u32[]{:S(2)}) collective-permute-start(f32[64,1,34,128]{3,0,2,1:T(8,128)S(1)} %get-tuple-element.8), channel_id=1, source_target_pairs={{1,0},{2,1},{3,2},{4,3},{5,4},{6,5},{7,6},{9,8},{10,9},{11,10},{12... | collective-permute-start | bytes 3342344 | tf_op jit(solution)/shard_map/ppermute | solution.py:15
where the time goes:
time: 275 us; the launch traced here: 274 us
  matrix products  73.1 us (27%)
  blocking collectives  51 us (19%)
  other arithmetic  47.8 us (17%)
  waiting for transfers between devices  41.5 us (15%)
  starting transfers between devices  31.1 us (11%)
  local copies, waits for them, and re-layouts  28.9 us (11%)
    dot_general x9, matrix products, convolve(): jnp.einsum('oi,ixyz->oxyz', weights[shift_x * 3 + shift_y], window, prefe...  64.8 us
    all_to_all x1, blocking collectives, on_device(): lax.all_to_all(partial_value, ('views', 'bricks'), split_axis=0, concat_a...  51 us
    concatenate x3, other arithmetic, padded_2(): array = jnp.concatenate([before, array, after], axis=dim)  25.4 us
    ppermute x4, waiting for transfers between devices, padded_2(): after = lax.ppermute(first, axis, down)  22.4 us
    ppermute x4, starting transfers between devices, padded_2(): before = lax.ppermute(last, axis, up)  17.3 us
    ppermute x4, waiting for transfers between devices, padded_2(): before = lax.ppermute(last, axis, up)  16.8 us
    convert_element_type x1, other arithmetic, on_device(): return smooth(beside_all, smooth_coef).astype(jnp.bfloat16)  11.6 us
    concatenate x1, other arithmetic, convolve(): jnp.concatenate([deep[..., 0:depth], deep[..., 1:depth + 1], deep[..., 2:...  9.4 us
  transfers between devices with their start and end apart: 9, of which 8 were waited for; matrix products, arithmetic and copies ran while one was open for 4% of the time, Pallas kernels for 0%

commit v1 on v0

v1 whole, which is shorter than its diff:
```python
import functools

import jax
import jax.numpy as jnp
from jax import lax
from jax.experimental import pallas as pl
from jax.experimental.pallas import tpu as pltpu
from jax.sharding import PartitionSpec as P

MESH = pl.DeviceIdType.MESH
DIRS = ((0, 1), (0, -1), (1, 0), (-1, 0), (1, 1), (1, -1), (-1, 1), (-1, -1))
LIMIT = 60 * 1024 * 1024


def lift_kernel(group, pixel_ref, ids_ref, feats_ref, tiles_ref, out_ref):
    step = pl.program_id(0)
    channels = feats_ref.shape[1]
    lanes = out_ref.shape[2]
    parts = tiles_ref.shape[2] // lanes
    for k in range(group):
        slot = step * group + k
        chosen = feats_ref[pixel_ref[slot]]
        value = jnp.dot(chosen, tiles_ref[k], preferred_element_type=jnp.float32)
        value = value.astype(jnp.bfloat16)
        for part in range(parts):
            out_ref[k, part * channels : (part + 1) * channels, :] = value[
                :, part * lanes : (part + 1) * lanes
            ]
        tail = out_ref.shape[1] - parts * channels
        ident = jnp.full((tail, lanes), ids_ref[slot], jnp.int32)
        out_ref[k, parts * channels :, :] = ident.astype(jnp.float32).astype(jnp.bfloat16)


def lift(pixel_ids, ids, feats, tiles, depth):
    slots, pixels, voxels = tiles.shape
    channels = feats.shape[1]
    group = 4
    rows = voxels // depth * channels + 8
    return pl.pallas_call(
        functools.partial(lift_kernel, group),
        out_shape=jax.ShapeDtypeStruct((slots, rows, depth), jnp.bfloat16),
        grid_spec=pltpu.PrefetchScalarGridSpec(
            num_scalar_prefetch=2,
            grid=(slots // group,),
            in_specs=[
                pl.BlockSpec(feats.shape, lambda i, *_: (0, 0, 0)),
                pl.BlockSpec((group, pixels, voxels), lambda i, *_: (i, 0, 0)),
            ],
            out_specs=pl.BlockSpec((group, rows, depth), lambda i, *_: (i, 0, 0)),
        ),
        name="lift",
    )(pixel_ids, ids, feats, tiles)


def scatter_kernel(ids_ref, got_ref, out_ref, acc):
    slots = got_ref.shape[0]
    blocks = out_ref.shape[0]
    rows = out_ref.shape[1]

    def clear(i, _):
        acc[i] = jnp.zeros(acc.shape[1:], jnp.float32)
        return 0

    def add(d, _):
        i = ids_ref[d]
        acc[i] = acc[i] + got_ref[d, 0:rows, :].astype(jnp.float32)
        return 0

    def put(i, _):
        out_ref[i] = jnp.maximum(acc[i], 0.0).astype(jnp.bfloat16)
        return 0

    lax.fori_loop(0, blocks, clear, 0)
    lax.fori_loop(0, slots, add, 0)
    lax.fori_loop(0, blocks, put, 0)


def scatter(ids, got, blocks):
    rows = got.shape[1] - 8
    depth = got.shape[2]
    return pl.pallas_call(
        scatter_kernel,
        out_shape=jax.ShapeDtypeStruct((blocks, rows, depth), jnp.bfloat16),
        grid_spec=pltpu.PrefetchScalarGridSpec(
            num_scalar_prefetch=1,
            grid=(1,),
            in_specs=[pl.BlockSpec(got.shape, lambda i, *_: (0, 0, 0))],
            out_specs=pl.BlockSpec((blocks, rows, depth), lambda i, *_: (0, 0, 0)),
            scratch_shapes=[pltpu.VMEM((blocks + 1, rows, depth), jnp.float32)],
        ),
        compiler_params=pltpu.CompilerParams(vmem_limit_bytes=LIMIT),
        name="scatter",
    )(ids, got)


def conv_kernel(
    views, bricks, r_ref, w_ref, bias_ref, coef_ref, out_ref,
    padded, stack, prod, gated, obuf, own_sem, send_sem, recv_sem, out_sem,
):
    v = lax.axis_index("views")
    b = lax.axis_index("bricks")
    size_x, size_y, ch, depth = r_ref.shape
    wide = 3 * ch

    def there(dv, db):
        return (v + dv >= 0) & (v + dv < views) & (b + db >= 0) & (b + db < bricks)

    def count(dv, db):
        return jnp.where(there(dv, db), 1, 0)

    own = pltpu.make_async_copy(
        r_ref, padded.at[pl.ds(2, size_x), pl.ds(2, size_y)], own_sem
    )
    own.start()

    barrier = pltpu.get_barrier_semaphore()
    total = 0
    for dv, db in DIRS:
        total = total + count(dv, db)

        @pl.when(there(dv, db))
        def _(dv=dv, db=db):
            pl.semaphore_signal(barrier, inc=1, device_id=(v + dv, b + db), device_id_type=MESH)

    pl.semaphore_wait(barrier, total)

    def span(delta, size):
        if delta == 0:
            return pl.ds(0, size), pl.ds(2, size)
        if delta == 1:
            return pl.ds(size - 2, 2), pl.ds(0, 2)
        return pl.ds(0, 2), pl.ds(size + 2, 2)

    def copy(k):
        dv, db = DIRS[k]
        from_x, to_x = span(db, size_x)
        from_y, to_y = span(dv, size_y)
        return pltpu.make_async_remote_copy(
            src_ref=r_ref.at[from_x, from_y],
            dst_ref=padded.at[to_x, to_y],
            send_sem=send_sem.at[k],
            recv_sem=recv_sem.at[k],
            device_id=(v + dv, b + db),
            device_id_type=MESH,
        )

    for k in range(len(DIRS)):
        dv, db = DIRS[k]

        @pl.when(there(dv, db))
        def _(k=k):
            copy(k).start()

    def receive(k):
        dv, db = DIRS[k]
        _, to_x = span(db, size_x)
        _, to_y = span(dv, size_y)

        @pl.when(there(-dv, -db))
        def _():
            copy(k).wait_recv()

        @pl.when(jnp.logical_not(there(-dv, -db)))
        def _():
            view = padded.at[to_x, to_y]
            view[...] = jnp.zeros(view.shape, jnp.bfloat16)

    def stack_plane(p):
        lane = lax.broadcasted_iota(jnp.int32, (ch, depth), 1)

        def row(y, _):
            at = pl.ds(pl.multiple_of(y * depth, depth), depth)
            here = padded[p, y]
            wide_here = here.astype(jnp.float32)
            before = jnp.where(lane == 0, 0.0, pltpu.roll(wide_here, 1, 1))
            after = jnp.where(lane == depth - 1, 0.0, pltpu.roll(wide_here, depth - 1, 1))
            base = p * wide
            stack[pl.ds(pl.multiple_of(base, ch), ch), at] = before.astype(jnp.bfloat16)
            stack[pl.ds(pl.multiple_of(base + ch, ch), ch), at] = here
            stack[pl.ds(pl.multiple_of(base + 2 * ch, ch), ch), at] = after.astype(jnp.bfloat16)
            return 0

        lax.fori_loop(0, size_y + 4, row, 0, unroll=4)

    lanes = 4 * depth
    chunks = (size_y + 4) // 4

    def conv_plane(g):
        rows = pl.ds(pl.multiple_of(g * wide, ch), 3 * wide)

        def chunk(c, _):
            at = pl.ds(pl.multiple_of(c * lanes, lanes), lanes)
            prod[:, at] = jnp.dot(w_ref[...], stack[rows, at], preferred_element_type=jnp.float32)
            return 0

        lax.fori_loop(0, chunks, chunk, 0, unroll=3)
        x = b * size_x + g - 1
        x_fits = (x >= 0) & (x < bricks * size_x)

        def row(y, _):
            at0 = pl.ds(pl.multiple_of(y * depth, depth), depth)
            at1 = pl.ds(pl.multiple_of((y + 1) * depth, depth), depth)
            at2 = pl.ds(pl.multiple_of((y + 2) * depth, depth), depth)
            value = prod[0:ch, at0] + prod[ch : 2 * ch, at1] + prod[2 * ch : wide, at2]
            value = jnp.maximum(value + bias_ref[...], 0.0)
            y_all = v * size_y + y - 1
            fits = x_fits & (y_all >= 0) & (y_all < views * size_y)
            gated[g, y] = value * jnp.where(fits, 1.0, 0.0)
            return 0

        lax.fori_loop(0, size_y + 2, row, 0, unroll=2)

    def loop(low, high, body):
        def step(i, _):
            body(i)
            return 0

        lax.fori_loop(low, high, step, 0)

    own.wait()
    receive(2)
    receive(3)
    loop(2, size_x + 2, stack_plane)
    loop(2, size_x, conv_plane)
    for k in (0, 1, 4, 5, 6, 7):
        receive(k)
    loop(0, 2, stack_plane)
    loop(size_x + 2, size_x + 4, stack_plane)
    loop(0, 2, conv_plane)
    loop(size_x, size_x + 2, conv_plane)

    def smooth_plane(x):
        lane = lax.broadcasted_iota(jnp.int32, (ch, depth), 1)

        def row(y, _):
            here = gated[x + 1, y + 1]
            beside = gated[x, y + 1] + gated[x + 2, y + 1] + gated[x + 1, y] + gated[x + 1, y + 2]
            before = jnp.where(lane == 0, 0.0, pltpu.roll(here, 1, 1))
            after = jnp.where(lane == depth - 1, 0.0, pltpu.roll(here, depth - 1, 1))
            beside = beside + before + after
            coef = coef_ref[x, pl.ds(y, 1), :]
            obuf[x, y] = (here + coef * (beside - 6.0 * here)).astype(jnp.bfloat16)
            return 0

        lax.fori_loop(0, size_y, row, 0, unroll=2)

    for x in range(size_x):
        smooth_plane(x)
        pltpu.make_async_copy(obuf.at[x], out_ref.at[x], out_sem.at[x]).start()
    for x in range(size_x):
        pltpu.make_async_copy(obuf.at[x], out_ref.at[x], out_sem.at[x]).wait()
    for k in range(len(DIRS)):
        dv, db = DIRS[k]

        @pl.when(there(dv, db))
        def _(k=k):
            copy(k).wait_send()


def convolve_smooth(rect, weights, bias, coef, views, bricks):
    size_x, size_y, ch, depth = rect.shape
    vmem = pl.BlockSpec(memory_space=pltpu.VMEM)
    anyspec = pl.BlockSpec(memory_space=pl.ANY)
    return pl.pallas_call(
        functools.partial(conv_kernel, views, bricks),
        out_shape=jax.ShapeDtypeStruct(rect.shape, jnp.bfloat16),
        in_specs=[anyspec, vmem, vmem, vmem],
        out_specs=anyspec,
        scratch_shapes=[
            pltpu.VMEM((size_x + 4, size_y + 4, ch, depth), jnp.bfloat16),
            pltpu.VMEM(((size_x + 4) * 3 * ch, (size_y + 4) * depth), jnp.bfloat16),
            pltpu.VMEM((3 * ch, (size_y + 4) * depth), jnp.float32),
            pltpu.VMEM((size_x + 2, size_y + 2, ch, depth), jnp.float32),
            pltpu.VMEM((size_x, size_y, ch, depth), jnp.bfloat16),
            pltpu.SemaphoreType.DMA,
            pltpu.SemaphoreType.DMA((len(DIRS),)),
            pltpu.SemaphoreType.DMA((len(DIRS),)),
            pltpu.SemaphoreType.DMA((size_x,)),
        ],
        compiler_params=pltpu.CompilerParams(
            collective_id=0, has_side_effects=True, vmem_limit_bytes=LIMIT
        ),
        name="conv",
    )(rect, weights, bias, coef)


def on_device(
    views, bricks,
    tile_pixel, tile_voxel, tile_count, features, interp, conv_weight, conv_bias, smooth_coef
):
    feats = features[0, 0]
    tiles = interp[0, 0]
    pixel_ids = tile_pixel[0, 0]
    voxel_ids = tile_voxel[0, 0]
    count = tile_count[0, 0]
    slots_total = tiles.shape[0]
    channels = feats.shape[1]
    size_x, size_y, depth = smooth_coef.shape
    per_block = tiles.shape[2] // depth
    blocks = size_x * size_y // per_block
    sender = lax.axis_index("views") * bricks + lax.axis_index("bricks")
    offset = jnp.remainder(sender * 37, slots_total)
    slot_ids = jnp.arange(slots_total, dtype=jnp.int32)
    live = jnp.remainder(slot_ids - offset, slots_total) < count
    ids = jnp.where(live, voxel_ids, blocks)
    partial = lift(pixel_ids, ids, feats, tiles, depth)
    got = lax.all_to_all(partial, ("views", "bricks"), split_axis=0, concat_axis=0, tiled=True)
    got_ids = got[:, got.shape[1] - 8, 0].astype(jnp.int32)
    rect = scatter(got_ids, got, blocks).reshape(size_x, size_y, channels, depth)
    weights = jnp.transpose(conv_weight, (1, 3, 0, 2, 4)).reshape(3 * channels, 9 * channels)
    bias = jnp.broadcast_to(conv_bias[:, None], (channels, depth))
    out = convolve_smooth(rect, weights, bias, smooth_coef, views, bricks)
    return jnp.transpose(out, (2, 0, 1, 3))


def solution(mesh):
    in_specs = (
        P("views", "bricks", None),
        P("views", "bricks", None),
        P("views", "bricks"),
        P("views", "bricks", None, None, None),
        P("views", "bricks", None, None, None),
        P(),
        P(),
        P("bricks", "views", None),
    )
    out_specs = P(None, "bricks", "views", None)
    body = functools.partial(on_device, mesh.shape["views"], mesh.shape["bricks"])
    return jax.shard_map(body, mesh=mesh, in_specs=in_specs, out_specs=out_specs, check_vma=False)
```

time: 275 us -> 144 us (0.52)
  Pallas kernels: 0 us -> 76.4 us
  matrix products: 73.1 us -> 0 us
  blocking collectives: 51 us -> 0 us
  other arithmetic: 47.8 us -> 2.49 us
  starting transfers between devices: 31.1 us -> 7.08 us
  local copies, waits for them, and re-layouts: 28.9 us -> 9.19 us
  waiting for transfers between devices: 41.5 us -> 47.9 us
    pallas_call x0 -> x3, Pallas kernels: none -> 76.4 us  [the longest x1 62.4 us: convolve_smooth(): pl.pallas_call(functools.partial(conv_kernel, views, bricks), out_shape=j...]
    dot_general x12 -> x0, matrix products: 73.1 us -> none  [the longest x9 64.8 us: convolve(): jnp.einsum('oi,ixyz->oxyz', weights[shift_x * 3 + shift_y], window, prefe...]
    all_to_all x1 -> x0, blocking collectives: 51 us -> none  [on_device(): lax.all_to_all(partial_value, ('views', 'bricks'), split_axis=0, concat_a...]
    all_to_all x1, waiting for transfers between devices: 2.34 us -> 47.9 us  [on_device(): lax.all_to_all(partial, ('views', 'bricks'), split_axis=0, concat_axis=0,...]
    ppermute x8 -> x0, waiting for transfers between devices: 39.2 us -> none  [the longest x4 22.4 us: padded_2(): after = lax.ppermute(first, axis, down)]
    concatenate x4 -> x0, other arithmetic: 34.8 us -> none  [the longest x3 25.4 us: padded_2(): array = jnp.concatenate([before, array, after], axis=dim)]
    ppermute x8 -> x0, starting transfers between devices: 24 us -> none  [the longest x4 17.3 us: padded_2(): before = lax.ppermute(last, axis, up)]
    convert_element_type x2 -> x0, local copies, waits for them, and re-layouts: 12.2 us -> none  [the longest x1 7.53 us: on_device(): rectified = jax.nn.relu(lifted).astype(jnp.bfloat16)]
  transfers between devices with their start and end apart: 9 -> 1, of which waited for: 8 -> 1; matrix products, arithmetic and copies ran while one was open for 4% -> 1% of each run, Pallas kernels for 0% -> 0%
where the time goes in v1:
time: 144 us
  Pallas kernels  76.4 us (53%)
  waiting for transfers between devices  47.9 us (33%)
  local copies, waits for them, and re-layouts  9.19 us (6%)
  starting transfers between devices  7.08 us (5%)
  other arithmetic  2.49 us (2%)
    pallas_call x1, Pallas kernels, convolve_smooth(): pl.pallas_call(functools.partial(conv_kernel, views, bricks), out_shape=j...  62.4 us
    all_to_all x1, waiting for transfers between devices, on_device(): lax.all_to_all(partial, ('views', 'bricks'), split_axis=0, concat_axis=0,...  47.9 us
    pallas_call x1, Pallas kernels, lift(): pl.pallas_call(functools.partial(lift_kernel, group), out_shape=jax.Shape...  7.67 us
    all_to_all x1, starting transfers between devices, on_device(): lax.all_to_all(partial, ('views', 'bricks'), split_axis=0, concat_axis=0,...  7.08 us
    transpose x1, local copies, waits for them, and re-layouts, on_device(): return jnp.transpose(out, (2, 0, 1, 3))  6.9 us
    pallas_call x1, Pallas kernels, scatter(): pl.pallas_call(scatter_kernel, out_shape=jax.ShapeDtypeStruct((blocks, ro...  6.28 us
  transfers between devices with their start and end apart: 1, of which 1 were waited for; matrix products, arithmetic and copies ran while one was open for 1% of the time, Pallas kernels for 0%

profile of v1, /device:TPU:1, one launch (start us, length us, event | category | flops | bytes accessed | tf_op | source)
XLA Modules:
  0.0 143.7 jit_solution(10311721858739919566)
XLA Ops:
  0.7 1.2 compare_select_fusion.2.ids_ref
  1.9 0.0 copy-start.1
  1.9 7.7 %lift.1 = bf16[32,264,128]{2,1,0:T(8,128)(2,1)} custom-call(s32[32]{0:T(128)} %bitcast.15, s32[32]{0:T(128)} %compare_select_fusion.2.ids_ref, bf16[16,64,128]{2,1,0:T(8,128)(2,1)} %bitcast.14, bf16[32,128,512]{2,1,0:T(8,128)(2,1)} %bitcast.12), custom_call_target="tpu_custom_call" | custom-call | tf_op jit(solution)/shard_map/lift/pallas_call | solution.py:39
  9.6 7.1 %all-to-all-start = ((bf16[32,264,128]{2,1,0:T(8,128)(2,1)}), bf16[32,264,128]{2,1,0:T(8,128)(2,1)S(1)}, u32[]{:S(2)}, u32[]{:S(2)}) async-start(bf16[32,264,128]{2,1,0:T(8,128)(2,1)} %lift.1), calls=%async_computation | async-start | bytes 4325376 | tf_op jit(solution)/shard_map/all_to_all | solution.py:307
  16.7 0.0 copy-start.2
  16.7 0.0 copy-done.1
  16.7 0.4 copy.11
  17.1 1.1 reshape.10.w_ref
  18.2 47.9 %all-to-all-done.got_ref = bf16[32,264,128]{2,1,0:T(8,128)(2,1)S(1)} async-done(((bf16[32,264,128]{2,1,0:T(8,128)(2,1)}), bf16[32,264,128]{2,1,0:T(8,128)(2,1)S(1)}, u32[]{:S(2)}, u32[]{:S(2)}) %all-to-all-start) | async-done | bytes 2162720 | tf_op jit(solution)/shard_map/all_to_all | solution.py:307
  66.1 0.0 copy-start
  66.1 1.2 fusion.ids_ref
  67.3 0.1 copy-done
  67.5 6.3 %scatter.1 = bf16[64,256,128]{2,1,0:T(8,128)(2,1)} custom-call(s32[32]{0:T(128)} %fusion.ids_ref, bf16[32,264,128]{2,1,0:T(8,128)(2,1)} %copy-done), custom_call_target="tpu_custom_call" | custom-call | tf_op jit(solution)/shard_map/scatter/pallas_call | solution.py:81
  73.8 0.0 copy-done.2
  73.8 0.7 broadcast_in_dim.11.bias_ref
  74.4 62.4 %conv.1 = bf16[8,32,64,128]{3,2,1,0:T(8,128)(2,1)} custom-call(bf16[8,32,64,128]{3,2,1,0:T(8,128)(2,1)} %bitcast.10, bf16[192,576]{1,0:T(8,128)(2,1)} %reshape.10.w_ref, f32[64,128]{1,0:T(8,128)} %broadcast_in_dim.11.bias_ref, f32[8,32,128]{2,1,0:T(8,128)} %coef_ref.1), custom_call_target="tpu_custom_call" | custom-call | tf_op jit(solution)/shard_map/conv/pallas_call | solution.py:264
  136.8 6.9 %copy.12 = bf16[64,8,32,128]{3,2,1,0:T(8,128)(2,1)} copy(bf16[64,8,32,128]{3,0,2,1:T(8,128)(2,1)} %bitcast.11) | data formatting | bytes 8388608 | tf_op jit(solution)/shard_map/transpose | solution.py:313
Async XLA Ops:
  1.9 14.8 %copy-start.1 = (bf16[3,3,3,64,64]{4,3,2,1,0:T(8,128)(2,1)S(1)}, bf16[3,3,3,64,64]{4,3,2,1,0:T(8,128)(2,1)}, u32[]{:S(2)}) copy-start(bf16[3,3,3,64,64]{4,3,2,1,0:T(8,128)(2,1)} %param.13) | copy-start | bytes 663556
  9.6 56.5 %all-to-all-start = ((bf16[32,264,128]{2,1,0:T(8,128)(2,1)}), bf16[32,264,128]{2,1,0:T(8,128)(2,1)S(1)}, u32[]{:S(2)}, u32[]{:S(2)}) async-start(bf16[32,264,128]{2,1,0:T(8,128)(2,1)} %lift.1), calls=%async_computation | async-start | bytes 4325376 | tf_op jit(solution)/shard_map/all_to_all | solution.py:307
  16.7 57.1 %copy-start.2 = (f32[64]{0:T(128)S(1)}, f32[64]{0:T(128)}, u32[]{:S(2)}) copy-start(f32[64]{0:T(128)} %param.14) | copy-start | bytes 772
  66.1 1.4 copy-start

commit v2 on v1

--- a/solution.py
+++ b/solution.py
@@ -9,6 +9,7 @@
 
 MESH = pl.DeviceIdType.MESH
 DIRS = ((0, 1), (0, -1), (1, 0), (-1, 0), (1, 1), (1, -1), (-1, 1), (-1, -1))
+GROUP = 4
 LIMIT = 60 * 1024 * 1024
 
 
@@ -95,7 +96,7 @@
 
 def conv_kernel(
     views, bricks, r_ref, w_ref, bias_ref, coef_ref, out_ref,
-    padded, stack, prod, gated, obuf, own_sem, send_sem, recv_sem, out_sem,
+    padded, prod, gated, obuf, own_sem, send_sem, recv_sem, out_sem,
 ):
     v = lax.axis_index("views")
     b = lax.axis_index("bricks")
@@ -165,50 +166,66 @@
             view = padded.at[to_x, to_y]
             view[...] = jnp.zeros(view.shape, jnp.bfloat16)
 
-    def stack_plane(p):
-        lane = lax.broadcasted_iota(jnp.int32, (ch, depth), 1)
-
-        def row(y, _):
-            at = pl.ds(pl.multiple_of(y * depth, depth), depth)
-            here = padded[p, y]
-            wide_here = here.astype(jnp.float32)
-            before = jnp.where(lane == 0, 0.0, pltpu.roll(wide_here, 1, 1))
-            after = jnp.where(lane == depth - 1, 0.0, pltpu.roll(wide_here, depth - 1, 1))
-            base = p * wide
-            stack[pl.ds(pl.multiple_of(base, ch), ch), at] = before.astype(jnp.bfloat16)
-            stack[pl.ds(pl.multiple_of(base + ch, ch), ch), at] = here
-            stack[pl.ds(pl.multiple_of(base + 2 * ch, ch), ch), at] = after.astype(jnp.bfloat16)
+    lane = lax.broadcasted_iota(jnp.int32, (ch, depth), 1)
+
+    def beside_z(low, high):
+        before = jnp.where(lane == 0, 0.0, pltpu.roll(low, 1, 1))
+        after = jnp.where(lane == depth - 1, 0.0, pltpu.roll(high, depth - 1, 1))
+        return before + after
+
+    def start_rows(slot, g, y):
+        tall = [
+            jnp.concatenate([padded[g + dx, y + dy + j] for j in range(GROUP)], axis=1)
+            for dx in range(3)
+            for dy in range(3)
+        ]
+        prod[slot] = jnp.dot(
+            w_ref[...], jnp.concatenate(tall, axis=0), preferred_element_type=jnp.float32
+        )
+
+    def finish_rows(slot, g, y):
+        x_all = b * size_x + g - 1
+        x_fits = (x_all >= 0) & (x_all < bricks * size_x)
+        for j in range(GROUP):
+            at = slice(j * depth, (j + 1) * depth)
+            value = prod[slot, ch : 2 * ch, at]
+            value = value + beside_z(prod[slot, 0:ch, at], prod[slot, 2 * ch : wide, at])
+            value = jnp.maximum(value + bias_ref[...], 0.0)
+            y_all = v * size_y + y + j - 1
+            fits = x_fits & (y_all >= 0) & (y_all < views * size_y)
+            gated[g, y + j] = value * jnp.where(fits, 1.0, 0.0)
+
+    def loop(low, high, body, unroll=1):
+        def step(i, _):
+            body(i)
             return 0
 
-        lax.fori_loop(0, size_y + 4, row, 0, unroll=4)
-
-    lanes = 4 * depth
-    chunks = (size_y + 4) // 4
-
-    def conv_plane(g):
-        rows = pl.ds(pl.multiple_of(g * wide, ch), 3 * wide)
-
-        def chunk(c, _):
-            at = pl.ds(pl.multiple_of(c * lanes, lanes), lanes)
-            prod[:, at] = jnp.dot(w_ref[...], stack[rows, at], preferred_element_type=jnp.float32)
-            return 0
-
-        lax.fori_loop(0, chunks, chunk, 0, unroll=3)
-        x = b * size_x + g - 1
-        x_fits = (x >= 0) & (x < bricks * size_x)
-
-        def row(y, _):
-            at0 = pl.ds(pl.multiple_of(y * depth, depth), depth)
-            at1 = pl.ds(pl.multiple_of((y + 1) * depth, depth), depth)
-            at2 = pl.ds(pl.multiple_of((y + 2) * depth, depth), depth)
-            value = prod[0:ch, at0] + prod[ch : 2 * ch, at1] + prod[2 * ch : wide, at2]
-            value = jnp.maximum(value + bias_ref[...], 0.0)
-            y_all = v * size_y + y - 1
-            fits = x_fits & (y_all >= 0) & (y_all < views * size_y)
-            gated[g, y] = value * jnp.where(fits, 1.0, 0.0)
-            return 0
-
-        lax.fori_loop(0, size_y + 2, row, 0, unroll=2)
+        lax.fori_loop(low, high, step, 0, unroll=unroll)
+
+    groups = size_y // GROUP
+
+    def smooth_rows(x, y):
+        here = gated[x + 1, y + 1]
+        beside = gated[x, y + 1] + gated[x + 2, y + 1] + gated[x + 1, y] + gated[x + 1, y + 2]
+        beside = beside + beside_z(here, here)
+        coef = coef_ref[x, pl.ds(y, 1), :]
+        obuf[x, y] = (here + coef * (beside - 6.0 * here)).astype(jnp.bfloat16)
+
+    def put(x):
+        pltpu.make_async_copy(obuf.at[x], out_ref.at[x], out_sem.at[x]).start()
+
+    def run_rows(g, starts, x=None):
+        for i, y in enumerate(starts):
+            start_rows(i % 2, g, y)
+            if x is not None:
+                for j in range(GROUP):
+                    if i * GROUP + j < size_y:
+                        smooth_rows(x, i * GROUP + j)
+            if i:
+                finish_rows((i - 1) % 2, g, starts[i - 1])
+        finish_rows((len(starts) - 1) % 2, g, starts[-1])
+        if x is not None:
+            put(x)
 
     def loop(low, high, body):
         def step(i, _):
@@ -217,36 +234,27 @@
 
         lax.fori_loop(low, high, step, 0)
 
+    middle = [GROUP * c for c in range(1, size_y // GROUP)]
+    ends = [0, size_y + 2 - GROUP]
+    rows = [0] + middle + [size_y + 2 - GROUP]
+
     own.wait()
+    loop(2, 5, lambda g: run_rows(g, middle))
     receive(2)
     receive(3)
-    loop(2, size_x + 2, stack_plane)
-    loop(2, size_x, conv_plane)
+    loop(2, 5, lambda g: run_rows(g, ends))
+    loop(5, size_x, lambda g: run_rows(g, rows, g - 3))
     for k in (0, 1, 4, 5, 6, 7):
         receive(k)
-    loop(0, 2, stack_plane)
-    loop(size_x + 2, size_x + 4, stack_plane)
-    loop(0, 2, conv_plane)
-    loop(size_x, size_x + 2, conv_plane)
-
-    def smooth_plane(x):
-        lane = lax.broadcasted_iota(jnp.int32, (ch, depth), 1)
-
-        def row(y, _):
-            here = gated[x + 1, y + 1]
-            beside = gated[x, y + 1] + gated[x + 2, y + 1] + gated[x + 1, y] + gated[x + 1, y + 2]
-            before = jnp.where(lane == 0, 0.0, pltpu.roll(here, 1, 1))
-            after = jnp.where(lane == depth - 1, 0.0, pltpu.roll(here, depth - 1, 1))
-            beside = beside + before + after
-            coef = coef_ref[x, pl.ds(y, 1), :]
-            obuf[x, y] = (here + coef * (beside - 6.0 * here)).astype(jnp.bfloat16)
-            return 0
-
-        lax.fori_loop(0, size_y, row, 0, unroll=2)
-
-    for x in range(size_x):
-        smooth_plane(x)
-        pltpu.make_async_copy(obuf.at[x], out_ref.at[x], out_sem.at[x]).start()
+    loop(size_x, size_x + 2, lambda g: run_rows(g, rows, g - 3))
+    loop(0, 2, lambda i: run_rows(1 - i, rows, jnp.where(i == 0, size_x - 1, 1)))
+
+    def first(y):
+        for j in range(GROUP):
+            smooth_rows(0, y * GROUP + j)
+
+    loop(0, size_y // GROUP, first)
+    put(0)
     for x in range(size_x):
         pltpu.make_async_copy(obuf.at[x], out_ref.at[x], out_sem.at[x]).wait()
     for k in range(len(DIRS)):
@@ -268,8 +276,7 @@
         out_specs=anyspec,
         scratch_shapes=[
             pltpu.VMEM((size_x + 4, size_y + 4, ch, depth), jnp.bfloat16),
-            pltpu.VMEM(((size_x + 4) * 3 * ch, (size_y + 4) * depth), jnp.bfloat16),
-            pltpu.VMEM((3 * ch, (size_y + 4) * depth), jnp.float32),
+            pltpu.VMEM((2, 3 * ch, GROUP * depth), jnp.float32),
             pltpu.VMEM((size_x + 2, size_y + 2, ch, depth), jnp.float32),
             pltpu.VMEM((size_x, size_y, ch, depth), jnp.bfloat16),
             pltpu.SemaphoreType.DMA,
@@ -307,7 +314,7 @@
     got = lax.all_to_all(partial, ("views", "bricks"), split_axis=0, concat_axis=0, tiled=True)
     got_ids = got[:, got.shape[1] - 8, 0].astype(jnp.int32)
     rect = scatter(got_ids, got, blocks).reshape(size_x, size_y, channels, depth)
-    weights = jnp.transpose(conv_weight, (1, 3, 0, 2, 4)).reshape(3 * channels, 9 * channels)
+    weights = jnp.transpose(conv_weight, (2, 3, 0, 1, 4)).reshape(3 * channels, 9 * channels)
     bias = jnp.broadcast_to(conv_bias[:, None], (channels, depth))
     out = convolve_smooth(rect, weights, bias, smooth_coef, views, bricks)
     return jnp.transpose(out, (2, 0, 1, 3))

time: 144 us -> 121 us (0.84); the launches traced: 144 us -> 119 us
  Pallas kernels: 76.4 us -> 51.6 us
    pallas_call x1, Pallas kernels: 62.4 us -> 37.6 us  [convolve_smooth(): pl.pallas_call(functools.partial(conv_kernel, views, bricks), out_shape=j...]
where the time goes in v2:
time: 121 us; the launch traced here: 119 us
  Pallas kernels  51.6 us (43%)
  waiting for transfers between devices  47.9 us (40%)
  local copies, waits for them, and re-layouts  9.19 us (8%)
  starting transfers between devices  7.08 us (6%)
  other arithmetic  2.49 us (2%)
    all_to_all x1, waiting for transfers between devices, on_device(): lax.all_to_all(partial, ('views', 'bricks'), split_axis=0, concat_axis=0,...  47.9 us
    pallas_call x1, Pallas kernels, convolve_smooth(): pl.pallas_call(functools.partial(conv_kernel, views, bricks), out_shape=j...  37.6 us
    pallas_call x1, Pallas kernels, lift(): pl.pallas_call(functools.partial(lift_kernel, group), out_shape=jax.Shape...  7.67 us
    all_to_all x1, starting transfers between devices, on_device(): lax.all_to_all(partial, ('views', 'bricks'), split_axis=0, concat_axis=0,...  7.08 us
    transpose x1, local copies, waits for them, and re-layouts, on_device(): return jnp.transpose(out, (2, 0, 1, 3))  6.9 us
    pallas_call x1, Pallas kernels, scatter(): pl.pallas_call(scatter_kernel, out_shape=jax.ShapeDtypeStruct((blocks, ro...  6.28 us
  transfers between devices with their start and end apart: 1, of which 1 were waited for; matrix products, arithmetic and copies ran while one was open for 1% of the time, Pallas kernels for 0%

profile of v2, /device:TPU:1, one launch (start us, length us, event | category | flops | bytes accessed | tf_op | source)
XLA Modules:
  0.0 118.9 jit_solution(8571349349284758590)
XLA Ops:
  0.7 1.2 %compare_select_fusion.2.ids_ref = s32[32]{0:T(128)} fusion(s32[1,1,32]{2,1,0:T(1,128)} %param.9, s32[]{:T(128)} %bitcast.9, s32[]{:T(128)S(6)} %select_n.17), kind=kLoop, calls=%fused_computation.4 | loop fusion | flops 448 | bytes 264 | tf_op jit(solution)/shard_map/jit(_where)/select_n | solution.py:312
  1.9 0.0 copy-start.1
  1.9 7.7 %lift.1 = bf16[32,264,128]{2,1,0:T(8,128)(2,1)} custom-call(s32[32]{0:T(128)} %bitcast.15, s32[32]{0:T(128)} %compare_select_fusion.2.ids_ref, bf16[16,64,128]{2,1,0:T(8,128)(2,1)} %bitcast.14, bf16[32,128,512]{2,1,0:T(8,128)(2,1)} %bitcast.12), custom_call_target="tpu_custom_call" | custom-call | tf_op jit(solution)/shard_map/lift/pallas_call | solution.py:40
  9.6 7.1 %all-to-all-start = ((bf16[32,264,128]{2,1,0:T(8,128)(2,1)}), bf16[32,264,128]{2,1,0:T(8,128)(2,1)S(1)}, u32[]{:S(2)}, u32[]{:S(2)}) async-start(bf16[32,264,128]{2,1,0:T(8,128)(2,1)} %lift.1), calls=%async_computation | async-start | bytes 4325376 | tf_op jit(solution)/shard_map/all_to_all | solution.py:314
  16.7 0.0 copy-start.2
  16.7 0.0 copy-done.1
  16.7 0.4 copy.11
  17.1 1.1 reshape.10.w_ref
  18.2 47.9 %all-to-all-done.got_ref = bf16[32,264,128]{2,1,0:T(8,128)(2,1)S(1)} async-done(((bf16[32,264,128]{2,1,0:T(8,128)(2,1)}), bf16[32,264,128]{2,1,0:T(8,128)(2,1)S(1)}, u32[]{:S(2)}, u32[]{:S(2)}) %all-to-all-start) | async-done | bytes 2162720 | tf_op jit(solution)/shard_map/all_to_all | solution.py:314
  66.1 0.0 copy-start
  66.1 1.2 %fusion.ids_ref = s32[32]{0:T(128)} fusion(bf16[32,264,128]{2,1,0:T(8,128)(2,1)S(1)} %all-to-all-done.got_ref), kind=kLoop, calls=%fused_computation.1 | loop fusion | flops 32 | bytes 192 | tf_op jit(solution)/shard_map/convert_element_type | solution.py:315
  67.3 0.1 copy-done
  67.5 6.3 %scatter.1 = bf16[64,256,128]{2,1,0:T(8,128)(2,1)} custom-call(s32[32]{0:T(128)} %fusion.ids_ref, bf16[32,264,128]{2,1,0:T(8,128)(2,1)} %copy-done), custom_call_target="tpu_custom_call" | custom-call | tf_op jit(solution)/shard_map/scatter/pallas_call | solution.py:82
  73.8 0.0 copy-done.2
  73.8 0.7 broadcast_in_dim.11.bias_ref
  74.4 37.6 %conv.1 = bf16[8,32,64,128]{3,2,1,0:T(8,128)(2,1)} custom-call(bf16[8,32,64,128]{3,2,1,0:T(8,128)(2,1)} %bitcast.10, bf16[192,576]{1,0:T(8,128)(2,1)} %reshape.10.w_ref, f32[64,128]{1,0:T(8,128)} %broadcast_in_dim.11.bias_ref, f32[8,32,128]{2,1,0:T(8,128)} %coef_ref.1), custom_call_target="tpu_custom_call" | custom-call | tf_op jit(solution)/shard_map/conv/pallas_call | solution.py:272
  112.0 6.9 %copy.12 = bf16[64,8,32,128]{3,2,1,0:T(8,128)(2,1)} copy(bf16[64,8,32,128]{3,0,2,1:T(8,128)(2,1)} %bitcast.11) | data formatting | bytes 8388608 | tf_op jit(solution)/shard_map/transpose | solution.py:320
Async XLA Ops:
  1.9 14.8 %copy-start.1 = (bf16[3,3,3,64,64]{4,3,2,1,0:T(8,128)(2,1)S(1)}, bf16[3,3,3,64,64]{4,3,2,1,0:T(8,128)(2,1)}, u32[]{:S(2)}) copy-start(bf16[3,3,3,64,64]{4,3,2,1,0:T(8,128)(2,1)} %param.13) | copy-start | bytes 663556
  9.6 56.5 %all-to-all-start = ((bf16[32,264,128]{2,1,0:T(8,128)(2,1)}), bf16[32,264,128]{2,1,0:T(8,128)(2,1)S(1)}, u32[]{:S(2)}, u32[]{:S(2)}) async-start(bf16[32,264,128]{2,1,0:T(8,128)(2,1)} %lift.1), calls=%async_computation | async-start | bytes 4325376 | tf_op jit(solution)/shard_map/all_to_all | solution.py:314
  16.7 57.1 %copy-start.2 = (f32[64]{0:T(128)S(1)}, f32[64]{0:T(128)}, u32[]{:S(2)}) copy-start(f32[64]{0:T(128)} %param.14) | copy-start | bytes 772
  66.1 1.4 %copy-start = (bf16[32,264,128]{2,1,0:T(8,128)(2,1)}, bf16[32,264,128]{2,1,0:T(8,128)(2,1)S(1)}, u32[]{:S(2)}) copy-start(bf16[32,264,128]{2,1,0:T(8,128)(2,1)S(1)} %all-to-all-done.got_ref) | copy-start | bytes 6488068

commit v3 on v2

--- a/solution.py
+++ b/solution.py
@@ -9,19 +9,27 @@
 
 MESH = pl.DeviceIdType.MESH
 DIRS = ((0, 1), (0, -1), (1, 0), (-1, 0), (1, 1), (1, -1), (-1, 1), (-1, -1))
+SENDS = (
+    (0, 1, 0), (0, -1, 0), (1, 0, None), (-1, 0, None),
+    (1, 1, None), (1, -1, None), (-1, 1, None), (-1, -1, None),
+    (0, 1, 1), (0, -1, 1),
+)
 GROUP = 4
 LIMIT = 60 * 1024 * 1024
 
 
-def lift_kernel(group, pixel_ref, ids_ref, feats_ref, tiles_ref, out_ref):
+def lift_kernel(pixel_ref, ids_ref, feats_ref, *refs):
+    streams, out_ref = refs[:-1], refs[-1]
+    each = streams[0].shape[0]
+    group = each * len(streams)
     step = pl.program_id(0)
     channels = feats_ref.shape[1]
     lanes = out_ref.shape[2]
-    parts = tiles_ref.shape[2] // lanes
+    parts = streams[0].shape[2] // lanes
     for k in range(group):
         slot = step * group + k
         chosen = feats_ref[pixel_ref[slot]]
-        value = jnp.dot(chosen, tiles_ref[k], preferred_element_type=jnp.float32)
+        value = jnp.dot(chosen, streams[k // each][k % each], preferred_element_type=jnp.float32)
         value = value.astype(jnp.bfloat16)
         for part in range(parts):
             out_ref[k, part * channels : (part + 1) * channels, :] = value[
@@ -35,22 +43,26 @@
 def lift(pixel_ids, ids, feats, tiles, depth):
     slots, pixels, voxels = tiles.shape
     channels = feats.shape[1]
-    group = 4
+    streams, each = 4, 2
+    group = streams * each
     rows = voxels // depth * channels + 8
     return pl.pallas_call(
-        functools.partial(lift_kernel, group),
+        lift_kernel,
         out_shape=jax.ShapeDtypeStruct((slots, rows, depth), jnp.bfloat16),
         grid_spec=pltpu.PrefetchScalarGridSpec(
             num_scalar_prefetch=2,
             grid=(slots // group,),
             in_specs=[
                 pl.BlockSpec(feats.shape, lambda i, *_: (0, 0, 0)),
-                pl.BlockSpec((group, pixels, voxels), lambda i, *_: (i, 0, 0)),
+            ]
+            + [
+                pl.BlockSpec((each, pixels, voxels), lambda i, *_, q=q: (i * streams + q, 0, 0))
+                for q in range(streams)
             ],
             out_specs=pl.BlockSpec((group, rows, depth), lambda i, *_: (i, 0, 0)),
         ),
         name="lift",
-    )(pixel_ids, ids, feats, tiles)
+    )(pixel_ids, ids, feats, *[tiles] * streams)
 
 
 def scatter_kernel(ids_ref, got_ref, out_ref, acc):
@@ -125,16 +137,20 @@
 
     pl.semaphore_wait(barrier, total)
 
-    def span(delta, size):
+    def span(delta, size, plane=None):
         if delta == 0:
             return pl.ds(0, size), pl.ds(2, size)
+        if plane is None:
+            low, width = 0, 2
+        else:
+            low, width = (1 - plane if delta == 1 else plane), 1
         if delta == 1:
-            return pl.ds(size - 2, 2), pl.ds(0, 2)
-        return pl.ds(0, 2), pl.ds(size + 2, 2)
+            return pl.ds(size - 2 + low, width), pl.ds(low, width)
+        return pl.ds(low, width), pl.ds(size + 2 + low, width)
 
     def copy(k):
-        dv, db = DIRS[k]
-        from_x, to_x = span(db, size_x)
+        dv, db, plane = SENDS[k]
+        from_x, to_x = span(db, size_x, plane)
         from_y, to_y = span(dv, size_y)
         return pltpu.make_async_remote_copy(
             src_ref=r_ref.at[from_x, from_y],
@@ -145,16 +161,15 @@
             device_id_type=MESH,
         )
 
-    for k in range(len(DIRS)):
-        dv, db = DIRS[k]
+    for k, (dv, db, _) in enumerate(SENDS):
 
         @pl.when(there(dv, db))
         def _(k=k):
             copy(k).start()
 
     def receive(k):
-        dv, db = DIRS[k]
-        _, to_x = span(db, size_x)
+        dv, db, plane = SENDS[k]
+        _, to_x = span(db, size_x, plane)
         _, to_y = span(dv, size_y)
 
         @pl.when(there(-dv, -db))
@@ -244,21 +259,42 @@
     receive(3)
     loop(2, 5, lambda g: run_rows(g, ends))
     loop(5, size_x, lambda g: run_rows(g, rows, g - 3))
-    for k in (0, 1, 4, 5, 6, 7):
-        receive(k)
-    loop(size_x, size_x + 2, lambda g: run_rows(g, rows, g - 3))
-    loop(0, 2, lambda i: run_rows(1 - i, rows, jnp.where(i == 0, size_x - 1, 1)))
-
-    def first(y):
+    low_first = b < bricks // 2
+
+    def boundary(i):
+        low_side = (i < 2) == low_first
+        odd = lax.rem(i, 2)
+        for db, side in ((1, low_side), (-1, jnp.logical_not(low_side))):
+            for plane in range(2):
+                keys = [
+                    k
+                    for k, (dv, step, part) in enumerate(SENDS)
+                    if step == db and (part == plane or (part is None and plane == 0))
+                ]
+
+                @pl.when(side & (odd == plane))
+                def _(keys=keys):
+                    for k in keys:
+                        receive(k)
+
+        g = jnp.where(low_side, 1 - odd, size_x + odd)
+        ahead = jnp.where(i == 1, 1, jnp.where(i == 2, 0, size_x - 2))
+        behind = jnp.where(i == 1, size_x - 2, jnp.where(i == 2, size_x - 1, 1))
+        x = jnp.where(i == 0, size_x - 3, jnp.where(low_first, ahead, behind))
+        run_rows(g, rows, x)
+
+    loop(0, 4, boundary)
+    last = jnp.where(low_first, size_x - 1, 0)
+
+    def finish(y):
         for j in range(GROUP):
-            smooth_rows(0, y * GROUP + j)
-
-    loop(0, size_y // GROUP, first)
-    put(0)
+            smooth_rows(last, y * GROUP + j)
+
+    loop(0, size_y // GROUP, finish)
+    put(last)
     for x in range(size_x):
         pltpu.make_async_copy(obuf.at[x], out_ref.at[x], out_sem.at[x]).wait()
-    for k in range(len(DIRS)):
-        dv, db = DIRS[k]
+    for k, (dv, db, _) in enumerate(SENDS):
 
         @pl.when(there(dv, db))
         def _(k=k):
@@ -280,8 +316,8 @@
             pltpu.VMEM((size_x + 2, size_y + 2, ch, depth), jnp.float32),
             pltpu.VMEM((size_x, size_y, ch, depth), jnp.bfloat16),
             pltpu.SemaphoreType.DMA,
-            pltpu.SemaphoreType.DMA((len(DIRS),)),
-            pltpu.SemaphoreType.DMA((len(DIRS),)),
+            pltpu.SemaphoreType.DMA((len(SENDS),)),
+            pltpu.SemaphoreType.DMA((len(SENDS),)),
             pltpu.SemaphoreType.DMA((size_x,)),
         ],
         compiler_params=pltpu.CompilerParams(

time: 121 us -> 113 us (0.934)
  Pallas kernels: 51.6 us -> 43.8 us
    pallas_call x1, Pallas kernels: 37.6 us -> 32 us  [convolve_smooth(): pl.pallas_call(functools.partial(conv_kernel, views, bricks), out_shape=j...]
    pallas_call x1, Pallas kernels: 7.67 us -> 5.5 us  [lift(): pl.pallas_call(lift_kernel, out_shape=jax.ShapeDtypeStruct((slots, rows,...]
where the time goes in v3:
time: 113 us; the launch traced here: 111 us
  waiting for transfers between devices  47.9 us (42%)
  Pallas kernels  43.8 us (39%)
  local copies, waits for them, and re-layouts  9.19 us (8%)
  starting transfers between devices  7.09 us (6%)
  other arithmetic  2.49 us (2%)
    all_to_all x1, waiting for transfers between devices, on_device(): lax.all_to_all(partial, ('views', 'bricks'), split_axis=0, concat_axis=0,...  47.9 us
    pallas_call x1, Pallas kernels, convolve_smooth(): pl.pallas_call(functools.partial(conv_kernel, views, bricks), out_shape=j...  32 us
    all_to_all x1, starting transfers between devices, on_device(): lax.all_to_all(partial, ('views', 'bricks'), split_axis=0, concat_axis=0,...  7.09 us
    transpose x1, local copies, waits for them, and re-layouts, on_device(): return jnp.transpose(out, (2, 0, 1, 3))  6.9 us
    pallas_call x1, Pallas kernels, scatter(): pl.pallas_call(scatter_kernel, out_shape=jax.ShapeDtypeStruct((blocks, ro...  6.28 us
    pallas_call x1, Pallas kernels, lift(): pl.pallas_call(lift_kernel, out_shape=jax.ShapeDtypeStruct((slots, rows,...  5.5 us
  transfers between devices with their start and end apart: 1, of which 1 were waited for; matrix products, arithmetic and copies ran while one was open for 1% of the time, Pallas kernels for 0%

profile of v3, /device:TPU:1, one launch (start us, length us, event | category | flops | bytes accessed | tf_op | source)
XLA Modules:
  0.0 111.2 jit_solution(13196439847093722020)
XLA Ops:
  0.7 1.2 %compare_select_fusion.2.ids_ref = s32[32]{0:T(128)} fusion(s32[1,1,32]{2,1,0:T(1,128)} %param.9, s32[]{:T(128)} %bitcast.9, s32[]{:T(128)S(6)} %select_n.17), kind=kLoop, calls=%fused_computation.4 | loop fusion | flops 448 | bytes 264 | tf_op jit(solution)/shard_map/jit(_where)/select_n | solution.py:348
  1.9 5.5 %lift.1 = bf16[32,264,128]{2,1,0:T(8,128)(2,1)} custom-call(s32[32]{0:T(128)} %bitcast.18, s32[32]{0:T(128)} %compare_select_fusion.2.ids_ref, bf16[16,64,128]{2,1,0:T(8,128)(2,1)} %bitcast.17, bf16[32,128,512]{2,1,0:T(8,128)(2,1)} %bitcast.10, bf16[32,128,512]{2,1,0:T(8,128)(2,1)} %bitcast.11, bf16[32,128,512]{2,1,0:T(8,128)(2,1)} %bitcast.12, ...), custom_call_target="tpu_custom_call" | custom-call | tf_op jit(solution)/shard_map/lift/pallas_call | solution.py:49
  7.4 0.0 copy-start.1
  7.4 7.1 %all-to-all-start = ((bf16[32,264,128]{2,1,0:T(8,128)(2,1)}), bf16[32,264,128]{2,1,0:T(8,128)(2,1)S(1)}, u32[]{:S(2)}, u32[]{:S(2)}) async-start(bf16[32,264,128]{2,1,0:T(8,128)(2,1)} %lift.1), calls=%async_computation | async-start | bytes 4325376 | tf_op jit(solution)/shard_map/all_to_all | solution.py:350
  14.5 0.0 copy-start.2
  14.5 0.0 copy-done.1
  14.5 0.4 copy.11
  14.9 1.1 reshape.10.w_ref
  16.0 47.9 %all-to-all-done.got_ref = bf16[32,264,128]{2,1,0:T(8,128)(2,1)S(1)} async-done(((bf16[32,264,128]{2,1,0:T(8,128)(2,1)}), bf16[32,264,128]{2,1,0:T(8,128)(2,1)S(1)}, u32[]{:S(2)}, u32[]{:S(2)}) %all-to-all-start) | async-done | bytes 2162720 | tf_op jit(solution)/shard_map/all_to_all | solution.py:350
  63.9 0.0 copy-start
  63.9 1.2 %fusion.ids_ref = s32[32]{0:T(128)} fusion(bf16[32,264,128]{2,1,0:T(8,128)(2,1)S(1)} %all-to-all-done.got_ref), kind=kLoop, calls=%fused_computation.1 | loop fusion | flops 32 | bytes 192 | tf_op jit(solution)/shard_map/convert_element_type | solution.py:351
  65.2 0.1 copy-done
  65.3 6.3 %scatter.1 = bf16[64,256,128]{2,1,0:T(8,128)(2,1)} custom-call(s32[32]{0:T(128)} %fusion.ids_ref, bf16[32,264,128]{2,1,0:T(8,128)(2,1)} %copy-done), custom_call_target="tpu_custom_call" | custom-call | tf_op jit(solution)/shard_map/scatter/pallas_call | solution.py:94
  71.6 0.0 copy-done.2
  71.6 0.7 broadcast_in_dim.11.bias_ref
  72.3 32.0 %conv.1 = bf16[8,32,64,128]{3,2,1,0:T(8,128)(2,1)} custom-call(bf16[8,32,64,128]{3,2,1,0:T(8,128)(2,1)} %bitcast.14, bf16[192,576]{1,0:T(8,128)(2,1)} %reshape.10.w_ref, f32[64,128]{1,0:T(8,128)} %broadcast_in_dim.11.bias_ref, f32[8,32,128]{2,1,0:T(8,128)} %coef_ref.1), custom_call_target="tpu_custom_call" | custom-call | tf_op jit(solution)/shard_map/conv/pallas_call | solution.py:308
  104.3 6.9 %copy.12 = bf16[64,8,32,128]{3,2,1,0:T(8,128)(2,1)} copy(bf16[64,8,32,128]{3,0,2,1:T(8,128)(2,1)} %bitcast.15) | data formatting | bytes 8388608 | tf_op jit(solution)/shard_map/transpose | solution.py:356
Async XLA Ops:
  7.4 7.1 %copy-start.1 = (bf16[3,3,3,64,64]{4,3,2,1,0:T(8,128)(2,1)S(1)}, bf16[3,3,3,64,64]{4,3,2,1,0:T(8,128)(2,1)}, u32[]{:S(2)}) copy-start(bf16[3,3,3,64,64]{4,3,2,1,0:T(8,128)(2,1)} %param.13) | copy-start | bytes 663556
  7.4 56.5 %all-to-all-start = ((bf16[32,264,128]{2,1,0:T(8,128)(2,1)}), bf16[32,264,128]{2,1,0:T(8,128)(2,1)S(1)}, u32[]{:S(2)}, u32[]{:S(2)}) async-start(bf16[32,264,128]{2,1,0:T(8,128)(2,1)} %lift.1), calls=%async_computation | async-start | bytes 4325376 | tf_op jit(solution)/shard_map/all_to_all | solution.py:350
  14.5 57.1 %copy-start.2 = (f32[64]{0:T(128)S(1)}, f32[64]{0:T(128)}, u32[]{:S(2)}) copy-start(f32[64]{0:T(128)} %param.14) | copy-start | bytes 772
  63.9 1.4 %copy-start = (bf16[32,264,128]{2,1,0:T(8,128)(2,1)}, bf16[32,264,128]{2,1,0:T(8,128)(2,1)S(1)}, u32[]{:S(2)}) copy-start(bf16[32,264,128]{2,1,0:T(8,128)(2,1)S(1)} %all-to-all-done.got_ref) | copy-start | bytes 6488068
